TPU v7x, 256 devices: a whole 4x4x8 slice. The times are simulated.
256 devices in a mesh: kx: 8 (over z), ht: 8 (over y, core), real: 4 (over x).
Axes of the slice: x: 4, y: 4, z: 8, core: 2. Of those that a mesh axis runs over, the one named last changes fastest.
Arguments:
- velocity: float32 [3, 4, 32, 512, 128], P(None, 'real', 'kx', 'ht'), may hold values from -6 to 6
- low_index: int32 [8], replicated, may hold values from 0 to 31, as said below
- neighbours: int32 [32, 8], P('kx'), may hold values from 0 to 31, as said below
- owner_map: int32 [64], replicated, may hold values from 0 to 63, each once
- mode_counts: int32 [32], P('kx'), may hold values from 16 to 64
- helmholtz: float32 [64, 512, 512], P(('kx', 'ht')), may hold values from -0.25 to 0.25
Outputs:
- velocity_next: float32 [3, 4, 32, 512, 128], P(None, 'real', 'kx', 'ht')
Inputs may be any that keep to these rules, and one draw needn't show every extreme that they name: `low_index`: distinct values. neighbours[m, j] lies within 4 modes of m, counting circularly over the 32 modes; offsets of + 4 and - 4 both occur.
All inputs are finite; a program needn't handle non-finite values.
Results may differ from a plain program's by a relative error of at most 0.0001.
Values sent between devices are 32-bit elements; how exact they have to be, the bound alone decides.
A program may use at most 64 MiB of HBM per device.

v0:
```python
import jax
import jax.numpy as jnp
from jax import lax
from jax.sharding import PartitionSpec as P

dt_step = 0.1


def extended_2(block, sides, width):
    for axis, dim in sides:
        count = lax.axis_size(axis)
        forward = [(i, i + 1) for i in range(count - 1)]
        forward.append((count - 1, 0))
        backward = [(target, source) for source, target in forward]
        low = lax.ppermute(
            lax.slice_in_dim(block, block.shape[dim] - width, None, axis=dim), axis, forward
        )
        high = lax.ppermute(lax.slice_in_dim(block, 0, width, axis=dim), axis, backward)
        block = jnp.concatenate([low, block, high], axis=dim)
    return block


def spanwise_tables(mode_count, point_count):
    column_ids = jnp.arange(2 * mode_count)
    wavenumber = (column_ids // 2).astype(jnp.float32)
    imag_part = column_ids % 2
    positions = 2.0 * jnp.pi * jnp.arange(point_count).astype(jnp.float32) / point_count
    phases = wavenumber[:, None] * positions[None, :]
    forward = jnp.where(imag_part[:, None] == 0, jnp.cos(phases), -jnp.sin(phases)) / jnp.sqrt(
        jnp.float32(mode_count)
    )
    backward = forward.T * (2.0 * mode_count / point_count)
    return (forward, backward)


def apply_inverse(block, helmholtz, kx_count, ht_count, slots_dev, rows_ht):
    components, reals_dev, band_modes = (block.shape[0], block.shape[1], block.shape[2])
    regrouped = block.reshape(
        components, reals_dev, band_modes, kx_count, ht_count, slots_dev, 2, rows_ht
    )
    regrouped = regrouped.transpose(0, 1, 3, 2, 5, 6, 4, 7)
    regrouped = regrouped.reshape(
        components, reals_dev, kx_count * band_modes, slots_dev, 2, ht_count * rows_ht
    )
    solved = jnp.einsum("syx,crmspx->crmspy", helmholtz, regrouped, precision=lax.Precision.HIGHEST)
    solved = solved.reshape(
        components, reals_dev, kx_count, band_modes, slots_dev, 2, ht_count, rows_ht
    )
    solved = solved.transpose(0, 1, 3, 2, 6, 4, 5, 7)
    return solved.reshape(block.shape)


def local(velocity, low_index, neighbours, owner_map, mode_counts, helmholtz):
    highest = lax.Precision.HIGHEST
    components, reals_dev, band_modes, rows_ht, columns = velocity.shape
    kz_modes = columns // 2
    forward, backward = spanwise_tables(kz_modes, 4 * kz_modes)
    kx_count = lax.axis_size("kx")
    ht_count = lax.axis_size("ht")
    kx_total = band_modes * kx_count
    realizations = reals_dev * lax.axis_size("real")
    owners = kx_count * ht_count
    slots_dev = kz_modes // owners
    width_out = slots_dev * 2 * rows_ht
    low_members = low_index.shape[0]
    band_start = lax.axis_index("kx") * band_modes
    global_modes = band_start + jnp.arange(band_modes, dtype=jnp.int32)
    low_select = (low_index[:, None] == global_modes[None, :]).astype(jnp.float32)
    high_mask = 1.0 - jnp.sum(low_select, axis=0)
    offsets = (neighbours - global_modes[:, None] + kx_total // 2) % kx_total - kx_total // 2
    local_partner = jnp.arange(band_modes, dtype=jnp.int32)[:, None] + band_modes + offsets
    column_mask = ((jnp.arange(columns) // 2)[None, :] < mode_counts[:, None]).astype(jnp.float32)
    inverse_map = (
        jnp.zeros((kz_modes,), jnp.int32).at[owner_map].set(jnp.arange(kz_modes, dtype=jnp.int32))
    )
    current = velocity
    physical = jnp.dot(current, forward, precision=highest)
    extended = extended_2(physical, (("kx", 2),), band_modes)
    own_low = jnp.einsum("jm,crmyz->crjyz", low_select, physical, precision=highest)
    low_fields = lax.psum(own_low, "kx")
    high_low = jnp.zeros_like(physical)
    stresses = []
    for member in range(low_members):
        partner = jnp.take(extended, local_partner[:, member], axis=2)
        low_one = low_fields[:, :, member : member + 1]
        high_low = high_low + low_one * partner[1:2] + partner * low_one[1:2]
        weighted = physical * (partner[1:2] * high_mask[None, None, :, None, None])
        stresses.append(jnp.sum(weighted, axis=(1, 2)))
    stress = jnp.stack(stresses, axis=1)
    nonlinear = jnp.dot(high_low, backward, precision=highest)
    summed = lax.psum(stress, ("kx", "real"))
    low_forcing = jnp.dot(summed / realizations, backward, precision=highest)
    forcing = nonlinear * high_mask[None, None, :, None, None]
    forcing = (
        forcing + jnp.einsum("jm,cjyk->cmyk", low_select, low_forcing, precision=highest)[:, None]
    )
    forcing = forcing * column_mask[None, None, :, None, :]
    updated = current + dt_step * forcing
    slotted = jnp.take(
        updated.reshape(components, reals_dev, band_modes, rows_ht, kz_modes, 2), owner_map, axis=4
    )
    outgoing = slotted.reshape(components, reals_dev, band_modes, rows_ht, owners, slots_dev, 2)
    outgoing = outgoing.transpose(0, 1, 2, 4, 5, 6, 3)
    flat_out = outgoing.reshape(components, reals_dev, band_modes, owners, width_out)
    applied = apply_inverse(
        lax.all_to_all(flat_out, ("kx", "ht"), split_axis=3, concat_axis=3, tiled=True),
        helmholtz,
        kx_count,
        ht_count,
        slots_dev,
        rows_ht,
    )
    returned = lax.all_to_all(applied, ("kx", "ht"), split_axis=3, concat_axis=3, tiled=True)
    restored = returned.reshape(components, reals_dev, band_modes, owners, slots_dev, 2, rows_ht)
    restored = restored.transpose(0, 1, 2, 6, 3, 4, 5).reshape(
        components, reals_dev, band_modes, rows_ht, kz_modes, 2
    )
    current = jnp.take(restored, inverse_map, axis=4).reshape(
        components, reals_dev, band_modes, rows_ht, columns
    )
    return current


def solution(mesh):
    in_specs = (
        P(None, "real", "kx", "ht", None),
        P(),
        P("kx", None),
        P(),
        P("kx"),
        P(("kx", "ht"), None, None),
    )
    out_specs = P(None, "real", "kx", "ht", None)
    return jax.shard_map(local, mesh=mesh, in_specs=in_specs, out_specs=out_specs, check_vma=False)
```

profile of v0, /device:TPU:1, one launch (start us, length us, event | category | flops | bytes accessed | tf_op | source)
XLA Modules:
  0.0 327.1 jit_solution(15920989410416831472)
XLA Ops:
  6.6 2.4 fusion.12
  9.0 2.5 collective-permute-start
  11.5 4.0 %collective-permute-start.1 = (f32[3,1,4,64,256]{4,3,2,0,1:T(8,128)S(1)}, f32[3,1,4,64,256]{4,3,2,0,1:T(8,128)}, u32[]{:S(2)}, u32[]{:S(2)}) collective-permute-start(f32[3,1,4,64,256]{4,3,2,0,1:T(8,128)S(1)} %bitcast.259), channel_id=1, source_target_pairs={{32,0},{64,32},{96,64},{128,96},{160,128},{192,160},{224,192},{0,2... | collective-permute-start | bytes 2359304 | tf_op jit(solution)/shard_map/ppermute | solution.py:18
  15.6 3.1 convolution_bitcast_fusion
  19.8 12.9 %collective-permute-done = f32[3,1,4,64,256]{4,3,2,0,1:T(8,128)S(1)} collective-permute-done((f32[3,1,4,64,256]{4,3,2,0,1:T(8,128)S(1)}, f32[3,1,4,64,256]{4,3,2,0,1:T(8,128)S(1)}, u32[]{:S(2)}, u32[]{:S(2)}) %collective-permute-start) | collective-permute-done | bytes 786464 | tf_op jit(solution)/shard_map/ppermute | solution.py:15
  33.6 1.8 maximum_bitcast_fusion
  35.4 1.6 gather_fusion.7
  37.0 1.5 gather_fusion.5
  38.5 1.5 gather_fusion.4
  40.0 1.5 gather_fusion.3
  41.5 1.5 gather_fusion.2
  43.0 1.5 gather_fusion.1
  46.0 1.5 gather_fusion.6
  55.4 3.9 %stack.35 = f32[3,8,64,256]{3,1,2,0:T(8,128)} concatenate(f32[3,1,64,256]{3,1,2,0:T(1,128)S(1)} %stack.27, f32[3,1,64,256]{3,1,2,0:T(1,128)S(1)} %stack.28, f32[3,1,64,256]{3,1,2,0:T(1,128)S(1)} %stack.29, f32[3,1,64,256]{3,1,2,0:T(1,128)S(1)} %stack.30, f32[3,1,64,256]{3,1,2,0:T(1,128)S(1)} %stack.31, f32[3,1,64,256]{3,1,2,0:T(1,128)S(1)} %stack.32, ...), dimensions={1} | concatenate | bytes 3145728 | tf_op jit(solution)/shard_map/stack | solution.py:89
  60.4 35.1 %all-reduce.3.cloned.1.call-done = f32[3,1,8,64,256]{4,2,3,0,1:T(8,128)} async-done(((f32[3,1,8,64,256]{4,2,3,0,1:T(8,128)}), f32[3,1,8,64,256]{4,2,3,0,1:T(8,128)}) %all-reduce.3.cloned.1.call-update) | async-done | bytes 1572880 | tf_op jit(solution)/shard_map/psum | solution.py:80
  95.5 7.7 %fusion.51 = (f32[3,1,1,64,256]{4,2,3,0,1:T(1,128)S(1)}, f32[3,1,1,64,256]{4,2,3,0,1:T(1,128)S(1)}, f32[3,1,1,64,256]{4,2,3,0,1:T(1,128)S(1)}, f32[3,1,1,64,256]...) fusion(f32[3,1,8,64,256]{4,2,3,0,1:T(8,128)} %all-reduce.3.clon, ...), kind=kLoop, calls=%fused_computation.172 | loop fusion | bytes 3145728 | tf_op jit(solution)/shard_map/slice | solution.py:85
  108.7 3.5 %fusion.52 = (f32[1,1,1,64,256]{4,2,3,0,1:T(1,128)S(1)}, f32[1,1,1,64,256]{4,2,3,0,1:T(1,128)S(1)}, f32[1,1,1,64,256]{4,2,3,0,1:T(1,128)S(1)}, f32[1,1,1,64,256]...) fusion(f32[3,1,8,64,256]{4,2,3,0,1:T(8,128)} %all-reduce.3.clon, ...), kind=kLoop, calls=%fused_computation.173 | loop fusion | bytes 1048576 | tf_op jit(solution)/shard_map/slice | solution.py:86
  116.0 133.7 %all-reduce.5.cloned.1.call-done = f32[3,8,64,256]{3,1,2,0:T(8,128)} async-done(((f32[3,8,64,256]{3,1,2,0:T(8,128)}), f32[3,8,64,256]{3,1,2,0:T(8,128)}) %all-reduce.5.cloned.1.call-update) | async-done | bytes 1572880 | tf_op jit(solution)/shard_map/psum | solution.py:91
  249.7 3.5 %fusion = f32[3,8,64,128]{3,1,2,0:T(8,128)S(1)} fusion(f32[3,8,64,256]{3,1,2,0:T(8,128)} %all-reduce.5.cloned.1.call-done, f32[256]{0:T(256)S(1)} %convert_multiply_fusion, f32[128]{0:T(128)} %copy-done.17, pred[128]{0:T(512)(128)(4,1)S(1)} %fusion.42), kind=kOutput, calls=%fused_computation.12 | convolution fusion | flops 604504064 | bytes 2360960 | tf_op jit(solution)/shard_map/dot_general | solution.py:92
  254.4 5.9 %fusion.6 = f32[3,1,4,64,128]{4,3,2,0,1:T(8,128)} fusion(f32[3,1,4,64,128]{4,3,2,1,0:T(8,128)S(1)} %copy-done.14, f32[3,64,128,4]{2,3,1,0:T(4,128)S(1)} %fusion.50, f32[4,128]{1,0:T(4,128)S(1)} %compare_convert_fusion.1, f32[4]{0:T(128)} %copy-done.27, f32[256]{0:T(256)S(1)} %convert_multiply_fusion, f32[128]{0:T(128)} %copy-done.17, ...), kind=kOutput, calls=%fused_computation.21 | convolution fusion | flops 310280192 | bytes 11669168 | tf_op jit(solution)/shard_map/dot_general | solution.py:90
  264.4 27.5 %all_to_all.10 = f32[3,1,4,64,128]{4,2,0,1,3:T(4,128)S(1)} all-to-all(f32[3,1,4,64,128]{4,2,0,1,3:T(4,128)S(1)} %reshape.457), channel_id=1, replica_groups=mesh['kx'=8,'ht'=8,'real'=4] {'kx','ht'}, dimensions={3} | all-to-all | bytes 786432 | tf_op jit(solution)/shard_map/all_to_all | solution.py:106
  292.8 1.5 convolution_bitcast_fusion.1
  296.2 5.5 %all-to-all-start.1 = ((f32[3,1,4,64,128]{4,2,0,1,3:T(4,128)}), f32[3,1,4,64,128]{4,2,0,1,3:T(4,128)S(1)}, u32[]{:S(2)}, u32[]{:S(2)}) async-start(f32[3,1,4,64,128]{4,2,0,1,3:T(4,128)} %reshape.459), calls=%async_computation.1 | async-start | bytes 786432 | tf_op jit(solution)/shard_map/all_to_all | solution.py:113
  302.6 14.2 %all-to-all-done.1 = f32[3,1,4,64,128]{4,2,0,1,3:T(4,128)S(1)} async-done(((f32[3,1,4,64,128]{4,2,0,1,3:T(4,128)}), f32[3,1,4,64,128]{4,2,0,1,3:T(4,128)S(1)}, u32[]{:S(2)}, u32[]{:S(2)}) %all-to-all-start.1) | async-done | bytes 393248 | tf_op jit(solution)/shard_map/all_to_all | solution.py:113
  (169 shorter events, 33.5 us)
Async XLA Ops:
  6.5 286.2 %copy-start = (f32[1,512,512]{2,1,0:T(8,128)S(1)}, f32[1,512,512]{2,1,0:T(8,128)}, u32[]{:S(2)}) copy-start(f32[1,512,512]{2,1,0:T(8,128)} %param.15) | copy-start | bytes 3145732
  6.5 89.0 %all-reduce.3.cloned.1.call-start = ((), (), s32[]{:S(2)}) async-start(), calls=%async_computation.2 | async-start | bytes 3145728 | tf_op jit(solution)/shard_map/psum | solution.py:80
  6.6 12.2 %copy-start.17 = (f32[128]{0:T(128)}, f32[128]{0:T(128)S(1)}, u32[]{:S(2)}) copy-start(f32[128]{0:T(128)S(1)} %fusion.45) | copy-start | bytes 1540
  6.6 12.2 %copy-start.28 = (s32[4,8]{1,0:T(4,128)S(1)}, s32[4,8]{1,0:T(4,128)}, u32[]{:S(2)}) copy-start(s32[4,8]{1,0:T(4,128)} %param.12) | copy-start | bytes 388
  6.6 13.0 %copy-start.29 = (s32[8]{0:T(128)S(1)}, s32[8]{0:T(128)}, u32[]{:S(2)}) copy-start(s32[8]{0:T(128)} %param.11) | copy-start | bytes 100
  9.0 23.7 %copy-start.1 = (f32[256,3,4,64]{0,3,2,1:T(8,128)}, f32[256,3,4,64]{0,3,2,1:T(8,128)S(1)}, u32[]{:S(2)}) copy-start(f32[256,3,4,64]{0,3,2,1:T(8,128)S(1)} %fusion.12) | copy-start | bytes 2359300
  9.0 23.7 %collective-permute-start = (f32[3,1,4,64,256]{4,3,2,0,1:T(8,128)S(1)}, f32[3,1,4,64,256]{4,3,2,0,1:T(8,128)S(1)}, u32[]{:S(2)}, u32[]{:S(2)}) collective-permute-start(f32[3,1,4,64,256]{4,3,2,0,1:T(8,128)S(1)} %bitcast.258), channel_id=1, source_target_pairs={{0,32},{32,64},{64,96},{96,128},{128,160},{160,192},{192,224},{224... | collective-permute-start | bytes 2359304 | tf_op jit(solution)/shard_map/ppermute | solution.py:15
  11.5 22.1 %collective-permute-start.1 = (f32[3,1,4,64,256]{4,3,2,0,1:T(8,128)S(1)}, f32[3,1,4,64,256]{4,3,2,0,1:T(8,128)}, u32[]{:S(2)}, u32[]{:S(2)}) collective-permute-start(f32[3,1,4,64,256]{4,3,2,0,1:T(8,128)S(1)} %bitcast.259), channel_id=1, source_target_pairs={{32,0},{64,32},{96,64},{128,96},{160,128},{192,160},{224,192},{0,2... | collective-permute-start | bytes 2359304 | tf_op jit(solution)/shard_map/ppermute | solution.py:18
  15.6 19.9 %copy-start.18 = (s32[4]{0:T(128)}, s32[4]{0:T(128)S(1)}, u32[]{:S(2)}) copy-start(s32[4]{0:T(128)S(1)} %get-tuple-element.70) | copy-start | bytes 52
  18.8 230.9 %all-reduce.5.cloned.1.call-start = ((), (), s32[]{:S(2)}) async-start(), calls=%async_computation.3 | async-start | bytes 3145728 | tf_op jit(solution)/shard_map/psum | solution.py:91
  19.2 28.2 %copy-start.19 = (pred[4]{0:T(512)(128)(4,1)}, pred[4]{0:T(512)(128)(4,1)S(1)}, u32[]{:S(2)}) copy-start(pred[4]{0:T(512)(128)(4,1)S(1)} %compare_and_fusion.2) | copy-start | bytes 16
  19.3 29.6 %copy-start.20 = (pred[4]{0:T(512)(128)(4,1)}, pred[4]{0:T(512)(128)(4,1)S(1)}, u32[]{:S(2)}) copy-start(pred[4]{0:T(512)(128)(4,1)S(1)} %compare_and_fusion.4) | copy-start | bytes 16
  19.3 30.9 %copy-start.21 = (pred[4]{0:T(512)(128)(4,1)}, pred[4]{0:T(512)(128)(4,1)S(1)}, u32[]{:S(2)}) copy-start(pred[4]{0:T(512)(128)(4,1)S(1)} %compare_and_fusion.5) | copy-start | bytes 16
  19.3 31.1 %copy-start.22 = (pred[4]{0:T(512)(128)(4,1)}, pred[4]{0:T(512)(128)(4,1)S(1)}, u32[]{:S(2)}) copy-start(pred[4]{0:T(512)(128)(4,1)S(1)} %compare_and_fusion.6) | copy-start | bytes 16
  19.4 31.2 %copy-start.23 = (pred[4]{0:T(512)(128)(4,1)}, pred[4]{0:T(512)(128)(4,1)S(1)}, u32[]{:S(2)}) copy-start(pred[4]{0:T(512)(128)(4,1)S(1)} %compare_and_fusion.7) | copy-start | bytes 16
  19.4 31.4 %copy-start.24 = (pred[4]{0:T(512)(128)(4,1)}, pred[4]{0:T(512)(128)(4,1)S(1)}, u32[]{:S(2)}) copy-start(pred[4]{0:T(512)(128)(4,1)S(1)} %compare_and_fusion.8) | copy-start | bytes 16
  19.7 31.8 %copy-start.25 = (pred[4]{0:T(512)(128)(4,1)}, pred[4]{0:T(512)(128)(4,1)S(1)}, u32[]{:S(2)}) copy-start(pred[4]{0:T(512)(128)(4,1)S(1)} %compare_and_fusion.9) | copy-start | bytes 16
  19.8 32.1 %copy-start.26 = (pred[4]{0:T(512)(128)(4,1)}, pred[4]{0:T(512)(128)(4,1)S(1)}, u32[]{:S(2)}) copy-start(pred[4]{0:T(512)(128)(4,1)S(1)} %compare_and_fusion.3) | copy-start | bytes 16
  19.8 32.3 %copy-start.27 = (f32[4]{0:T(128)}, f32[4]{0:T(128)S(1)}, u32[]{:S(2)}) copy-start(f32[4]{0:T(128)S(1)} %broadcast_subtract_fusion) | copy-start | bytes 52
  55.4 5.0 %copy-start.32 = (s32[4]{0:T(128)S(1)}, s32[4]{0:T(128)}, u32[]{:S(2)}) copy-start(s32[4]{0:T(128)} %param.14) | copy-start | bytes 52
  112.2 142.2 %copy-start.3 = (f32[4,3,64,256]{3,2,1,0:T(8,128)S(1)}, f32[4,3,64,256]{3,2,1,0:T(8,128)}, u32[]{:S(2)}) copy-start(f32[4,3,64,256]{3,2,1,0:T(8,128)} %gather_fusion.7) | copy-start | bytes 2359300
  112.2 142.2 %copy-start.4 = (f32[4,3,64,256]{3,2,1,0:T(8,128)S(1)}, f32[4,3,64,256]{3,2,1,0:T(8,128)}, u32[]{:S(2)}) copy-start(f32[4,3,64,256]{3,2,1,0:T(8,128)} %gather_fusion.5) | copy-start | bytes 2359300
  249.7 4.7 %copy-start.15 = (f32[4,64,256]{2,1,0:T(8,128)S(1)}, f32[4,64,256]{2,1,0:T(8,128)}, u32[]{:S(2)}) copy-start(f32[4,64,256]{2,1,0:T(8,128)} %get-tuple-element.40) | copy-start | bytes 786436
  296.2 20.6 %all-to-all-start.1 = ((f32[3,1,4,64,128]{4,2,0,1,3:T(4,128)}), f32[3,1,4,64,128]{4,2,0,1,3:T(4,128)S(1)}, u32[]{:S(2)}, u32[]{:S(2)}) async-start(f32[3,1,4,64,128]{4,2,0,1,3:T(4,128)} %reshape.459), calls=%async_computation.1 | async-start | bytes 786432 | tf_op jit(solution)/shard_map/all_to_all | solution.py:113
  (15 other events, 38.1 us)
Sparse Core Ops, SparseCore 0:
  18.9 76.5 all-reduce.2
  98.9 150.7 all-reduce.4
where the time goes:
time: 328 us; the launch traced here: 327 us
  waiting for transfers between devices  196 us (60%)
  local copies, waits for them, and re-layouts  50.8 us (15%)
  blocking collectives  27.5 us (8%)
  matrix products  17.6 us (5%)
  between operations  14.4 us (4%)
  starting transfers between devices  12.1 us (4%)
  other arithmetic  8.77 us (3%)
    psum x1, waiting for transfers between devices, local(): summed = lax.psum(stress, ('kx', 'real'))  134 us
    psum x1, waiting for transfers between devices, local(): low_fields = lax.psum(own_low, 'kx')  35.1 us
    all_to_all x1, blocking collectives, local(): lax.all_to_all(flat_out, ('kx', 'ht'), split_axis=3, concat_axis=3, tiled...  27.5 us
    all_to_all x1, waiting for transfers between devices, local(): lax.all_to_all(applied, ('kx', 'ht'), split_axis=3, concat_axis=3, tiled=...  14.2 us
    ppermute x1, waiting for transfers between devices, extended_2(): lax.ppermute(lax.slice_in_dim(block, block.shape[dim] - width, None, axis...  12.9 us
    gather x8, local copies, waits for them, and re-layouts, local(): partner = jnp.take(extended, local_partner[:, member], axis=2)  12 us
    unnamed x84, local copies, waits for them, and re-layouts  11.8 us
    slice x1, local copies, waits for them, and re-layouts, local(): low_one = low_fields[:, :, member:member + 1]  7.67 us
  transfers between devices with their start and end apart: 5, of which 4 were waited for; matrix products, arithmetic and copies ran while one was open for 15% of the time, Pallas kernels for 0%

commit v1 on v0

--- a/solution.py
+++ b/solution.py
@@ -110,7 +110,9 @@
         slots_dev,
         rows_ht,
     )
-    returned = lax.all_to_all(applied, ("kx", "ht"), split_axis=3, concat_axis=3, tiled=True)
+    pieces = jnp.split(applied, lax.axis_size(("kx", "ht")), axis=3)
+    received = lax.all_to_all(jnp.stack(pieces), ("kx", "ht"), 0, 0)
+    returned = jnp.concatenate(received, axis=3)
     restored = returned.reshape(components, reals_dev, band_modes, owners, slots_dev, 2, rows_ht)
     restored = restored.transpose(0, 1, 2, 6, 3, 4, 5).reshape(
         components, reals_dev, band_modes, rows_ht, kz_modes, 2

time: 328 us -> 365 us (1.11)
  local copies, waits for them, and re-layouts: 50.8 us -> 87.6 us
    unnamed x84 -> x151, local copies, waits for them, and re-layouts: 11.8 us -> 48.8 us
  transfers between devices with their start and end apart: 5 -> 5, of which waited for: 4 -> 4; matrix products, arithmetic and copies ran while one was open for 15% -> 14% of each run, Pallas kernels for 0% -> 0%
where the time goes in v1:
time: 365 us; the launch traced here: 364 us
  waiting for transfers between devices  196 us (54%)
  local copies, waits for them, and re-layouts  87.6 us (24%)
  blocking collectives  27.5 us (8%)
  matrix products  17.6 us (5%)
  between operations  14.5 us (4%)
  starting transfers between devices  12.1 us (3%)
  other arithmetic  8.73 us (2%)
    psum x1, waiting for transfers between devices, local(): summed = lax.psum(stress, ('kx', 'real'))  134 us
    unnamed x151, local copies, waits for them, and re-layouts  48.8 us
    psum x1, waiting for transfers between devices, local(): low_fields = lax.psum(own_low, 'kx')  34.3 us
    all_to_all x1, blocking collectives, local(): lax.all_to_all(flat_out, ('kx', 'ht'), split_axis=3, concat_axis=3, tiled...  27.5 us
    all_to_all x1, waiting for transfers between devices, local(): received = lax.all_to_all(jnp.stack(pieces), ('kx', 'ht'), 0, 0)  15.1 us
    ppermute x1, waiting for transfers between devices, extended_2(): lax.ppermute(lax.slice_in_dim(block, block.shape[dim] - width, None, axis...  12.9 us
    gather x8, local copies, waits for them, and re-layouts, local(): partner = jnp.take(extended, local_partner[:, member], axis=2)  12 us
    slice x1, local copies, waits for them, and re-layouts, local(): low_one = low_fields[:, :, member:member + 1]  7.67 us
  transfers between devices with their start and end apart: 5, of which 4 were waited for; matrix products, arithmetic and copies ran while one was open for 14% of the time, Pallas kernels for 0%

profile of v1, /device:TPU:1, one launch (start us, length us, event | category | flops | bytes accessed | tf_op | source)
XLA Modules:
  0.0 364.1 jit_solution(2653898044586742558)
XLA Ops:
  6.6 2.4 fusion.12
  9.1 2.5 collective-permute-start
  11.6 4.0 %collective-permute-start.1 = (f32[3,1,4,64,256]{4,3,2,0,1:T(8,128)S(1)}, f32[3,1,4,64,256]{4,3,2,0,1:T(8,128)}, u32[]{:S(2)}, u32[]{:S(2)}) collective-permute-start(f32[3,1,4,64,256]{4,3,2,0,1:T(8,128)S(1)} %bitcast.450), channel_id=1, source_target_pairs={{32,0},{64,32},{96,64},{128,96},{160,128},{192,160},{224,192},{0,2... | collective-permute-start | bytes 2359304 | tf_op jit(solution)/shard_map/ppermute | solution.py:18
  15.6 3.1 convolution_bitcast_fusion
  19.8 12.9 %collective-permute-done = f32[3,1,4,64,256]{4,3,2,0,1:T(8,128)S(1)} collective-permute-done((f32[3,1,4,64,256]{4,3,2,0,1:T(8,128)S(1)}, f32[3,1,4,64,256]{4,3,2,0,1:T(8,128)S(1)}, u32[]{:S(2)}, u32[]{:S(2)}) %collective-permute-start) | collective-permute-done | bytes 786464 | tf_op jit(solution)/shard_map/ppermute | solution.py:15
  33.7 1.8 maximum_bitcast_fusion
  35.5 1.6 gather_fusion.7
  37.0 1.5 gather_fusion.5
  38.6 1.5 gather_fusion.4
  40.1 1.5 gather_fusion.3
  41.5 1.5 gather_fusion.2
  43.1 1.5 gather_fusion.1
  46.0 1.5 gather_fusion.6
  55.4 3.7 %stack.230 = f32[3,8,64,256]{3,1,2,0:T(8,128)} concatenate(f32[3,1,64,256]{3,1,2,0:T(1,128)S(1)} %stack.222, f32[3,1,64,256]{3,1,2,0:T(1,128)S(1)} %stack.223, f32[3,1,64,256]{3,1,2,0:T(1,128)S(1)} %stack.224, f32[3,1,64,256]{3,1,2,0:T(1,128)S(1)} %stack.225, f32[3,1,64,256]{3,1,2,0:T(1,128)S(1)} %stack.226, f32[3,1,64,256]{3,1,2,0:T(1,128)S(1)} %stack.227, ...), dimensions={1} | concatenate | bytes 3145728 | tf_op jit(solution)/shard_map/stack | solution.py:89
  60.7 34.3 %all-reduce.3.cloned.1.call-done = f32[3,1,8,64,256]{4,2,3,0,1:T(8,128)} async-done(((f32[3,1,8,64,256]{4,2,3,0,1:T(8,128)}), f32[3,1,8,64,256]{4,2,3,0,1:T(8,128)}) %all-reduce.3.cloned.1.call-update) | async-done | bytes 1572880 | tf_op jit(solution)/shard_map/psum | solution.py:80
  95.0 7.7 %fusion.51 = (f32[3,1,1,64,256]{4,2,3,0,1:T(1,128)S(1)}, f32[3,1,1,64,256]{4,2,3,0,1:T(1,128)S(1)}, f32[3,1,1,64,256]{4,2,3,0,1:T(1,128)S(1)}, f32[3,1,1,64,256]...) fusion(f32[3,1,8,64,256]{4,2,3,0,1:T(8,128)} %all-reduce.3.clon, ...), kind=kLoop, calls=%fused_computation.236 | loop fusion | bytes 3145728 | tf_op jit(solution)/shard_map/slice | solution.py:85
  108.2 3.5 fusion.52
  115.5 133.7 %all-reduce.5.cloned.1.call-done = f32[3,8,64,256]{3,1,2,0:T(8,128)} async-done(((f32[3,8,64,256]{3,1,2,0:T(8,128)}), f32[3,8,64,256]{3,1,2,0:T(8,128)}) %all-reduce.5.cloned.1.call-update) | async-done | bytes 1572880 | tf_op jit(solution)/shard_map/psum | solution.py:91
  249.2 3.5 fusion
  254.0 5.9 %fusion.6 = f32[3,1,4,64,128]{4,3,2,0,1:T(8,128)} fusion(f32[3,1,4,64,128]{4,3,2,1,0:T(8,128)S(1)} %copy-done.14, f32[3,64,128,4]{2,3,1,0:T(4,128)S(1)} %fusion.50, f32[4,128]{1,0:T(4,128)S(1)} %compare_convert_fusion.1, f32[4]{0:T(128)} %copy-done.28, f32[256]{0:T(256)S(1)} %convert_multiply_fusion, f32[128]{0:T(128)} %copy-done.18, ...), kind=kOutput, calls=%fused_computation.21 | convolution fusion | flops 310280192 | bytes 11669168 | tf_op jit(solution)/shard_map/dot_general | solution.py:90
  264.0 27.5 %all_to_all.10 = f32[3,1,4,64,128]{4,2,0,1,3:T(4,128)S(1)} all-to-all(f32[3,1,4,64,128]{4,2,0,1,3:T(4,128)S(1)} %reshape.457), channel_id=1, replica_groups=mesh['kx'=8,'ht'=8,'real'=4] {'kx','ht'}, dimensions={3} | all-to-all | bytes 786432 | tf_op jit(solution)/shard_map/all_to_all | solution.py:106
  292.3 1.5 convolution_bitcast_fusion.1
  333.2 5.4 %all-to-all-start.1 = ((f32[64,3,1,4,1,128]{5,3,1,4,2,0:T(4,128)}), f32[64,3,1,4,1,128]{5,3,1,4,2,0:T(4,128)S(1)}, u32[]{:S(2)}, u32[]{:S(2)}) async-start(f32[64,3,1,4,1,128]{5,3,1,4,2,0:T(4,128)} %constant_dynamic-update-slice_fusion), calls=%async_computation.1 | async-start | bytes 786432 | tf_op jit(solution)/shard_map/all_to_all | solution.py:114
  338.7 15.1 %all-to-all-done.1 = f32[64,3,1,4,1,128]{5,3,1,4,2,0:T(4,128)S(1)} async-done(((f32[64,3,1,4,1,128]{5,3,1,4,2,0:T(4,128)}), f32[64,3,1,4,1,128]{5,3,1,4,2,0:T(4,128)S(1)}, u32[]{:S(2)}, u32[]{:S(2)}) %all-to-all-start.1) | async-done | bytes 393248 | tf_op jit(solution)/shard_map/all_to_all | solution.py:114
  (240 shorter events, 70.5 us)
Async XLA Ops:
  6.5 285.8 %copy-start = (f32[1,512,512]{2,1,0:T(8,128)S(1)}, f32[1,512,512]{2,1,0:T(8,128)}, u32[]{:S(2)}) copy-start(f32[1,512,512]{2,1,0:T(8,128)} %param.15) | copy-start | bytes 3145732
  6.5 88.5 %all-reduce.3.cloned.1.call-start = ((), (), s32[]{:S(2)}) async-start(), calls=%async_computation.2 | async-start | bytes 3145728 | tf_op jit(solution)/shard_map/psum | solution.py:80
  6.6 12.3 %copy-start.29 = (s32[4,8]{1,0:T(4,128)S(1)}, s32[4,8]{1,0:T(4,128)}, u32[]{:S(2)}) copy-start(s32[4,8]{1,0:T(4,128)} %param.12) | copy-start | bytes 388
  6.6 13.0 %copy-start.30 = (s32[8]{0:T(128)S(1)}, s32[8]{0:T(128)}, u32[]{:S(2)}) copy-start(s32[8]{0:T(128)} %param.11) | copy-start | bytes 100
  6.6 13.2 %copy-start.33 = (s32[64]{0:T(128)S(1)}, s32[64]{0:T(128)}, u32[]{:S(2)}) copy-start(s32[64]{0:T(128)} %param.13) | copy-start | bytes 772
  9.0 23.7 %copy-start.1 = (f32[256,3,4,64]{0,3,2,1:T(8,128)}, f32[256,3,4,64]{0,3,2,1:T(8,128)S(1)}, u32[]{:S(2)}) copy-start(f32[256,3,4,64]{0,3,2,1:T(8,128)S(1)} %fusion.12) | copy-start | bytes 2359300
  9.1 23.7 %collective-permute-start = (f32[3,1,4,64,256]{4,3,2,0,1:T(8,128)S(1)}, f32[3,1,4,64,256]{4,3,2,0,1:T(8,128)S(1)}, u32[]{:S(2)}, u32[]{:S(2)}) collective-permute-start(f32[3,1,4,64,256]{4,3,2,0,1:T(8,128)S(1)} %bitcast.449), channel_id=1, source_target_pairs={{0,32},{32,64},{64,96},{96,128},{128,160},{160,192},{192,224},{224... | collective-permute-start | bytes 2359304 | tf_op jit(solution)/shard_map/ppermute | solution.py:15
  11.6 22.1 %collective-permute-start.1 = (f32[3,1,4,64,256]{4,3,2,0,1:T(8,128)S(1)}, f32[3,1,4,64,256]{4,3,2,0,1:T(8,128)}, u32[]{:S(2)}, u32[]{:S(2)}) collective-permute-start(f32[3,1,4,64,256]{4,3,2,0,1:T(8,128)S(1)} %bitcast.450), channel_id=1, source_target_pairs={{32,0},{64,32},{96,64},{128,96},{160,128},{192,160},{224,192},{0,2... | collective-permute-start | bytes 2359304 | tf_op jit(solution)/shard_map/ppermute | solution.py:18
  15.6 19.9 %copy-start.19 = (s32[4]{0:T(128)}, s32[4]{0:T(128)S(1)}, u32[]{:S(2)}) copy-start(s32[4]{0:T(128)S(1)} %get-tuple-element.134) | copy-start | bytes 52
  18.8 230.4 %all-reduce.5.cloned.1.call-start = ((), (), s32[]{:S(2)}) async-start(), calls=%async_computation.3 | async-start | bytes 3145728 | tf_op jit(solution)/shard_map/psum | solution.py:91
  19.3 28.2 %copy-start.20 = (pred[4]{0:T(512)(128)(4,1)}, pred[4]{0:T(512)(128)(4,1)S(1)}, u32[]{:S(2)}) copy-start(pred[4]{0:T(512)(128)(4,1)S(1)} %compare_and_fusion.2) | copy-start | bytes 16
  19.3 29.6 %copy-start.21 = (pred[4]{0:T(512)(128)(4,1)}, pred[4]{0:T(512)(128)(4,1)S(1)}, u32[]{:S(2)}) copy-start(pred[4]{0:T(512)(128)(4,1)S(1)} %compare_and_fusion.4) | copy-start | bytes 16
  19.3 31.0 %copy-start.22 = (pred[4]{0:T(512)(128)(4,1)}, pred[4]{0:T(512)(128)(4,1)S(1)}, u32[]{:S(2)}) copy-start(pred[4]{0:T(512)(128)(4,1)S(1)} %compare_and_fusion.5) | copy-start | bytes 16
  19.4 31.1 %copy-start.23 = (pred[4]{0:T(512)(128)(4,1)}, pred[4]{0:T(512)(128)(4,1)S(1)}, u32[]{:S(2)}) copy-start(pred[4]{0:T(512)(128)(4,1)S(1)} %compare_and_fusion.6) | copy-start | bytes 16
  19.4 31.2 %copy-start.24 = (pred[4]{0:T(512)(128)(4,1)}, pred[4]{0:T(512)(128)(4,1)S(1)}, u32[]{:S(2)}) copy-start(pred[4]{0:T(512)(128)(4,1)S(1)} %compare_and_fusion.7) | copy-start | bytes 16
  19.4 31.4 %copy-start.25 = (pred[4]{0:T(512)(128)(4,1)}, pred[4]{0:T(512)(128)(4,1)S(1)}, u32[]{:S(2)}) copy-start(pred[4]{0:T(512)(128)(4,1)S(1)} %compare_and_fusion.8) | copy-start | bytes 16
  19.5 32.1 %copy-start.26 = (pred[4]{0:T(512)(128)(4,1)}, pred[4]{0:T(512)(128)(4,1)S(1)}, u32[]{:S(2)}) copy-start(pred[4]{0:T(512)(128)(4,1)S(1)} %compare_and_fusion.9) | copy-start | bytes 16
  19.8 32.1 %copy-start.27 = (pred[4]{0:T(512)(128)(4,1)}, pred[4]{0:T(512)(128)(4,1)S(1)}, u32[]{:S(2)}) copy-start(pred[4]{0:T(512)(128)(4,1)S(1)} %compare_and_fusion.3) | copy-start | bytes 16
  19.8 32.3 %copy-start.28 = (f32[4]{0:T(128)}, f32[4]{0:T(128)S(1)}, u32[]{:S(2)}) copy-start(f32[4]{0:T(128)S(1)} %broadcast_subtract_fusion) | copy-start | bytes 52
  60.1 45.3 %copy-start.34 = (s32[64]{0:T(128)}, s32[64]{0:T(128)S(1)}, u32[]{:S(2)}) copy-start(s32[64]{0:T(128)S(1)} %scatter_custom_fusion) | copy-start | bytes 772
  111.7 142.3 %copy-start.3 = (f32[4,3,64,256]{3,2,1,0:T(8,128)S(1)}, f32[4,3,64,256]{3,2,1,0:T(8,128)}, u32[]{:S(2)}) copy-start(f32[4,3,64,256]{3,2,1,0:T(8,128)} %gather_fusion.7) | copy-start | bytes 2359300
  111.7 142.3 %copy-start.4 = (f32[4,3,64,256]{3,2,1,0:T(8,128)S(1)}, f32[4,3,64,256]{3,2,1,0:T(8,128)}, u32[]{:S(2)}) copy-start(f32[4,3,64,256]{3,2,1,0:T(8,128)} %gather_fusion.5) | copy-start | bytes 2359300
  293.8 44.9 %copy-start.35 = (s32[64]{0:T(128)S(1)}, s32[64]{0:T(128)}, u32[]{:S(2)}) copy-start(s32[64]{0:T(128)} %copy-done.34) | copy-start | bytes 772
  333.2 20.6 %all-to-all-start.1 = ((f32[64,3,1,4,1,128]{5,3,1,4,2,0:T(4,128)}), f32[64,3,1,4,1,128]{5,3,1,4,2,0:T(4,128)S(1)}, u32[]{:S(2)}, u32[]{:S(2)}) async-start(f32[64,3,1,4,1,128]{5,3,1,4,2,0:T(4,128)} %constant_dynamic-update-slice_fusion), calls=%async_computation.1 | async-start | bytes 786432 | tf_op jit(solution)/shard_map/all_to_all | solution.py:114
  (17 other events, 48.8 us)
Sparse Core Ops, SparseCore 0:
  18.9 76.0 all-reduce.2
  98.4 150.7 all-reduce.4
